TPU v7x, 512 devices: a whole 4x4x16 slice. The times are simulated.
512 devices in a mesh: group: 4 (over x), shard: 32 (over z, y_hi), tensor: 4 (over y_lo, core).
Axes of the slice: x: 4, y: 4 (y_hi: 2, y_lo: 2; y = y_hi * 2 + y_lo), z: 16, core: 2. Of those that a mesh axis runs over, the one named last changes fastest.
Arguments:
- deltas: bfloat16 [4, 2048, 2048], P('group', None, 'tensor'), may hold values from -6 to 6
- factor: bfloat16 [2048, 64], P('tensor'), may hold values from -0.29882812 to 0.29882812
- master: float32 [2048, 2048], P(('group', 'shard'), 'tensor'), may hold values from -6 to 6
- momentum: float32 [2048, 2048], P(('group', 'shard'), 'tensor'), may hold values from -3 to 3
Outputs:
- new_master: float32 [2048, 2048], P(('group', 'shard'), 'tensor')
- new_momentum: float32 [2048, 2048], P(('group', 'shard'), 'tensor')
- weights: bfloat16 [2048, 2048], P(None, 'tensor')
All inputs are finite; a program needn't handle non-finite values.
Results may differ from a plain program's by a relative error of at most 0.009.
Values may be sent and summed in bfloat16 or wider, within the bound.
A program may use at most 64 MiB of HBM per device.

v0:
```python
import jax
import jax.numpy as jnp
from jax import lax
from jax.sharding import PartitionSpec as P

momentum_rate = 0.9
outer_rate = 0.7


def shards(deltas, factor, master, momentum):
    group_count = lax.axis_size("group")
    shard_count = lax.axis_size("shard")
    shard_index = lax.axis_index("shard")
    row_count = master.shape[0]
    col_count = master.shape[1]
    own_delta = deltas[0]
    blocks = own_delta.reshape(group_count, shard_count, row_count, col_count)
    picked = lax.dynamic_index_in_dim(blocks, shard_index, 1, keepdims=False)
    factor_wide = factor.astype(jnp.float32)
    summed = lax.psum_scatter(
        picked.astype(jnp.float32).astype(jnp.bfloat16), "group", scatter_dimension=0, tiled=True
    ).astype(jnp.float32)
    partial_value = jnp.dot(summed[0], factor_wide, precision=lax.Precision.HIGHEST)
    coefficients = lax.psum(partial_value, "tensor")
    outer_grad = (
        lax.dot_general(
            coefficients, factor_wide, (((1,), (1,)), ((), ())), precision=lax.Precision.HIGHEST
        )
        / group_count
    )
    new_momentum = momentum_rate * momentum + outer_grad
    new_master = master - outer_rate * (outer_grad + momentum_rate * new_momentum)
    fresh_copy = new_master.astype(jnp.bfloat16)
    weights = lax.all_gather(fresh_copy, ("group", "shard"), axis=0, tiled=True)
    return (new_master, new_momentum, weights)


def solution(mesh):
    return jax.shard_map(
        shards,
        mesh=mesh,
        in_specs=(
            P("group", None, "tensor"),
            P("tensor", None),
            P(("group", "shard"), "tensor"),
            P(("group", "shard"), "tensor"),
        ),
        out_specs=(
            P(("group", "shard"), "tensor"),
            P(("group", "shard"), "tensor"),
            P(None, "tensor"),
        ),
        check_vma=False,
    )
```

profile of v0, /device:TPU:2, one launch (start us, length us, event | category | flops | bytes accessed | tf_op | source)
XLA Modules:
  0.0 274.1 jit_solution(17234697237845103731)
XLA Ops:
  7.2 0.0 copy-start
  7.2 0.0 reduce-scatter.2.cloned.1.call-start
  7.2 1.5 copy-done
  8.8 0.6 dynamic-slice_bitcast_fusion
  9.4 0.0 reduce-scatter.2.cloned.1.call-update
  9.4 0.0 all-gather.2.cloned.1.call-start
  9.5 33.2 %reduce-scatter.2.cloned.1.call-done = bf16[1,16,512]{2,1,0:T(8,128)(2,1)} async-done(((bf16[4,16,512]{2,1,0:T(8,128)(2,1)}), bf16[1,16,512]{2,1,0:T(8,128)(2,1)}) %reduce-scatter.2.cloned.1.call-update) | async-done | bytes 16400 | tf_op jit(solution)/shard_map/reduce_scatter | solution.py:20
  42.7 1.0 fusion
  43.7 5.7 %psum.7 = f32[16,64]{1,0:T(8,128)S(1)} all-reduce(f32[16,64]{1,0:T(8,128)S(1)} %fusion), channel_id=1, replica_groups=mesh['group'=4,'shard'=32,'tensor'=4] {'tensor'}, use_global_device_ids=true, to_apply=%region_1.2 | all-reduce | flops 1024 | bytes 8192 | tf_op jit(solution)/shard_map/psum | solution.py:24
  49.4 1.6 fusion.2
  51.1 0.0 all-gather.2.cloned.1.call-update
  51.1 213.1 %all-gather.2.cloned.1.call-done = bf16[2048,512]{1,0:T(8,128)(2,1)} async-done(((bf16[16,512]{1,0:T(8,128)(2,1)}), bf16[2048,512]{1,0:T(8,128)(2,1)}) %all-gather.2.cloned.1.call-update) | async-done | bytes 2097168 | tf_op jit(solution)/shard_map/all_gather | solution.py:34
  264.2 3.0 %copy.8 = bf16[2048,512]{1,0:T(8,128)(2,1)} copy(bf16[2048,512]{1,0:T(8,128)(2,1)} %all-gather.2.cloned.1.call-done) | data formatting | bytes 4194304
Async XLA Ops:
  7.2 1.6 copy-start
  7.2 35.5 %reduce-scatter.2.cloned.1.call-start = ((), (), s32[]{:S(2)}) async-start(), calls=%async_computation.1 | async-start | bytes 81920 | tf_op jit(solution)/shard_map/reduce_scatter | solution.py:20
  9.4 254.8 %all-gather.2.cloned.1.call-start = ((), (), s32[]{:S(2)}) async-start(), calls=%async_computation.2 | async-start | bytes 2113536 | tf_op jit(solution)/shard_map/all_gather | solution.py:34
Sparse Core Ops, SparseCore 0:
  11.4 31.2 reduce-scatter.1
  51.2 212.9 all-gather.1
where the time goes:
time: 274 us
  waiting for transfers between devices  246 us (90%)
  between operations  14.1 us (5%)
  blocking collectives  5.75 us (2%)
  local copies, waits for them, and re-layouts  5.22 us (2%)
    all_gather x1, waiting for transfers between devices, shards(): weights = lax.all_gather(fresh_copy, ('group', 'shard'), axis=0, tiled=True)  213 us
    reduce_scatter x1, waiting for transfers between devices, shards(): lax.psum_scatter(picked.astype(jnp.float32).astype(jnp.bfloat16), 'group'...  33.2 us
    psum x1, blocking collectives, shards(): coefficients = lax.psum(partial_value, 'tensor')  5.75 us
  transfers between devices with their start and end apart: 2, of which 2 were waited for; matrix products, arithmetic and copies ran while one was open for 0% of the time, Pallas kernels for 0%

commit v1 on v0

--- a/solution.py
+++ b/solution.py
@@ -1,3 +1,4 @@
+import functools
 import jax
 import jax.numpy as jnp
 from jax import lax
@@ -5,6 +6,15 @@
 
 momentum_rate = 0.9
 outer_rate = 0.7
+
+
+def _spread_strings(here_x, bus_axis):
+    return jnp.concatenate(
+        lax.all_to_all(jnp.stack([here_x] * lax.axis_size(bus_axis)), bus_axis, 0, 0), 0
+    )
+
+
+records_make = functools.partial(_spread_strings, bus_axis=("group", "shard"))
 
 
 def shards(deltas, factor, master, momentum):
@@ -31,7 +41,7 @@
     new_momentum = momentum_rate * momentum + outer_grad
     new_master = master - outer_rate * (outer_grad + momentum_rate * new_momentum)
     fresh_copy = new_master.astype(jnp.bfloat16)
-    weights = lax.all_gather(fresh_copy, ("group", "shard"), axis=0, tiled=True)
+    weights = records_make(fresh_copy)
     return (new_master, new_momentum, weights)
 
 

time: 274 us -> 179 us (0.65)
  waiting for transfers between devices: 246 us -> 33.3 us
  blocking collectives: 5.75 us -> 125 us
    all_gather x1 -> x0, waiting for transfers between devices: 213 us -> none  [shards(): weights = lax.all_gather(fresh_copy, ('group', 'shard'), axis=0, tiled=True)]
    all_to_all x0 -> x1, blocking collectives: none -> 119 us  [_spread_strings(): lax.all_to_all(jnp.stack([here_x] * lax.axis_size(bus_axis)), bus_axis, 0...]
  transfers between devices with their start and end apart: 2 -> 1, of which waited for: 2 -> 1; matrix products, arithmetic and copies ran while one was open for 0% -> 0% of each run, Pallas kernels for 0% -> 0%
where the time goes in v1:
time: 179 us; the launch traced here: 178 us
  blocking collectives  125 us (70%)
  waiting for transfers between devices  33.3 us (19%)
  between operations  14.1 us (8%)
  local copies, waits for them, and re-layouts  3.74 us (2%)
  matrix products  2.62 us (1%)
    all_to_all x1, blocking collectives, _spread_strings(): lax.all_to_all(jnp.stack([here_x] * lax.axis_size(bus_axis)), bus_axis, 0...  119 us
    reduce_scatter x1, waiting for transfers between devices, shards(): lax.psum_scatter(picked.astype(jnp.float32).astype(jnp.bfloat16), 'group'...  33.3 us
    psum x1, blocking collectives, shards(): coefficients = lax.psum(partial_value, 'tensor')  5.75 us
  transfers between devices with their start and end apart: 1, of which 1 were waited for; matrix products, arithmetic and copies ran while one was open for 0% of the time, Pallas kernels for 0%

profile of v1, /device:TPU:2, one launch (start us, length us, event | category | flops | bytes accessed | tf_op | source)
XLA Modules:
  0.0 178.3 jit_solution(14444260581980952074)
XLA Ops:
  7.2 0.0 copy-start
  7.2 0.0 reduce-scatter.2.cloned.1.call-start
  7.2 1.5 copy-done
  8.8 0.6 dynamic-slice_bitcast_fusion
  9.4 0.0 reduce-scatter.2.cloned.1.call-update
  9.4 33.3 %reduce-scatter.2.cloned.1.call-done = bf16[1,16,512]{2,1,0:T(8,128)(2,1)} async-done(((bf16[4,16,512]{2,1,0:T(8,128)(2,1)}), bf16[1,16,512]{2,1,0:T(8,128)(2,1)}) %reduce-scatter.2.cloned.1.call-update) | async-done | bytes 16400 | tf_op jit(solution)/shard_map/reduce_scatter | solution.py:30
  42.7 1.0 fusion
  43.7 5.7 %psum.7 = f32[16,64]{1,0:T(8,128)S(1)} all-reduce(f32[16,64]{1,0:T(8,128)S(1)} %fusion), channel_id=1, replica_groups=mesh['group'=4,'shard'=32,'tensor'=4] {'tensor'}, use_global_device_ids=true, to_apply=%region_1.2 | all-reduce | flops 1024 | bytes 8192 | tf_op jit(solution)/shard_map/psum | solution.py:34
  49.4 1.6 fusion.2
  51.1 0.2 stack.2
  51.3 118.8 %all_to_all.5 = bf16[128,16,512]{2,1,0:T(8,128)(2,1)S(1)} all-to-all(bf16[128,16,512]{2,1,0:T(8,128)(2,1)S(1)} %stack.2), channel_id=1, replica_groups=mesh['group'=4,'shard'=32,'tensor'=4] {'group','shard'}, dimensions={0} | all-to-all | bytes 4194304 | tf_op jit(solution)/shard_map/all_to_all | solution.py:13
  170.1 1.3 copy.8
Async XLA Ops:
  7.2 1.6 copy-start
  7.2 35.5 %reduce-scatter.2.cloned.1.call-start = ((), (), s32[]{:S(2)}) async-start(), calls=%async_computation.2 | async-start | bytes 81920 | tf_op jit(solution)/shard_map/reduce_scatter | solution.py:30
Sparse Core Ops, SparseCore 0:
  11.4 31.2 reduce-scatter.1
